TPU v7x, 32 devices: a whole 2x2x4 slice. The times are simulated.
32 devices in a mesh: row: 4 (over y, x), col: 8 (over z, core).
Axes of the slice: x: 2, y: 2, z: 4, core: 2. Of those that a mesh axis runs over, the one named last changes fastest.
Arguments:
- new_row: float32 [128, 96, 128], P('row', 'col'), may hold values from -4 to 4
- history: float32 [96, 96, 128, 128], P('row', 'col'), may hold values from -0.0546875 to 0.0546875
- hamiltonian: float32 [128, 128], replicated, may hold values from -0.5 to 0.5
Outputs:
- rows_out: float32 [3, 128, 96, 128], P(None, 'row', 'col')
All inputs are finite; a program needn't handle non-finite values.
Results may differ from a plain program's by a relative error of at most 0.00026.
Values sent between devices are 32-bit elements; how exact they have to be, the bound alone decides.
No kernel may reach another device: no remote copies, remote signals or barrier semaphores. Data moves between devices by JAX's collectives and lax.ppermute only.
A program may use at most 128 MiB of HBM per device.

v0:
```python
import jax
import jax.numpy as jnp
from jax import lax
from jax.sharding import PartitionSpec as P

STEPS = 3


time_step = 0.2


def sigma_panel(sigma_all, tile_rows):
    row_start = lax.axis_index("row") * tile_rows
    pieces = lax.all_to_all(sigma_all, "col", split_axis=0, concat_axis=1, tiled=True)
    needed = lax.dynamic_slice_in_dim(pieces, row_start, tile_rows, 1)
    return lax.all_gather(needed, "col", axis=0, tiled=True)


def contract(sigma_rows, history):
    return jnp.einsum(
        "isl,stlj->itj",
        sigma_rows,
        history,
        precision=lax.Precision.HIGHEST,
        preferred_element_type=jnp.float32,
    )


def advance(current, hamiltonian, collision):
    kinetic = jnp.einsum(
        "itl,lj->itj",
        current,
        hamiltonian,
        precision=lax.Precision.HIGHEST,
        preferred_element_type=jnp.float32,
    )
    return current - time_step * (kinetic + collision)


def per_device(new_row, history, hamiltonian):
    tile_rows = history.shape[0]
    results = []
    current = new_row
    for step_index in range(STEPS):
        sigma_local = current * current * current
        sigma_all = lax.all_gather(sigma_local, "row", axis=0, tiled=True)
        sigma_rows = sigma_panel(sigma_all, tile_rows)
        collision = lax.psum_scatter(
            contract(sigma_rows, history), "row", scatter_dimension=0, tiled=True
        )
        current = advance(current, hamiltonian, collision)
        results.append(current)
    return jnp.stack(results)


def solution(mesh):
    placed = (P("row", "col", None), P("row", "col", None, None), P())
    return jax.shard_map(
        per_device,
        mesh=mesh,
        in_specs=placed,
        out_specs=P(None, "row", "col", None),
        check_vma=False,
    )
```

profile of v0, /device:TPU:0, one launch (start us, length us, event | category | flops | bytes accessed | tf_op | source)
XLA Modules:
  0.0 342.0 jit_solution(1827196471069993955)
XLA Ops:
  6.5 0.0 copy-start
  6.5 1.0 multiply_multiply_fusion.2
  7.5 12.7 %all_gather.18 = f32[128,12,128]{2,0,1:T(8,128)S(1)} all-gather(f32[32,12,128]{2,0,1:T(8,128)S(1)} %multiply_multiply_fusion.2), channel_id=1, replica_groups=mesh['row'=4,'col'=8] {'row'}, dimensions={0}, use_global_device_ids=true | all-gather | bytes 983040 | tf_op jit(solution)/shard_map/all_gather | solution.py:46
  20.2 1.5 copy.21
  21.6 4.9 %all-to-all-start = ((f32[128,12,128]{2,1,0:T(8,128)}), f32[128,12,128]{2,1,0:T(8,128)S(1)}, u32[]{:S(2)}, u32[]{:S(2)}) async-start(f32[128,12,128]{2,1,0:T(8,128)} %copy.21), calls=%async_computation | async-start | bytes 2097152 | tf_op jit(solution)/shard_map/all_to_all | solution.py:14
  26.5 0.0 all-gather.4.cloned.1.call-start
  26.6 26.5 %all-to-all-done = f32[128,12,128]{2,1,0:T(8,128)S(1)} async-done(((f32[128,12,128]{2,1,0:T(8,128)}), f32[128,12,128]{2,1,0:T(8,128)S(1)}, u32[]{:S(2)}, u32[]{:S(2)}) %all-to-all-start) | async-done | bytes 786464 | tf_op jit(solution)/shard_map/all_to_all | solution.py:14
  53.1 0.2 copy.22
  53.3 0.7 constant_dynamic-slice_fusion.2
  54.0 0.0 all-gather.4.cloned.1.call-update
  54.1 0.0 copy-start.1
  54.1 0.0 reduce-scatter.4.cloned.1.call-start
  54.1 23.3 %all-gather.4.cloned.1.call-done = f32[128,24,128]{2,0,1:T(8,128)} async-done(((f32[16,24,128]{2,0,1:T(8,128)}), f32[128,24,128]{2,0,1:T(8,128)}) %all-gather.4.cloned.1.call-update) | async-done | bytes 1572880 | tf_op jit(solution)/shard_map/all_gather | solution.py:16
  77.5 14.3 %fusion.6 = f32[128,12,128]{2,0,1:T(8,128)} fusion(f32[24,12,128,128]{3,2,1,0:T(8,128)} %param.4, f32[128,24,128]{2,0,1:T(8,128)} %all-gather.4.cloned.1.call-done), kind=kOutput, calls=%fused_computation.6 | convolution fusion | flops 7247757312 | bytes 21233664 | tf_op jit(solution)/shard_map/isl,stlj->itj/dot_general | solution.py:20
  91.7 0.0 reduce-scatter.4.cloned.1.call-update
  91.7 0.0 all-gather.6.cloned.1.call-start
  91.8 25.4 %reduce-scatter.4.cloned.1.call-done = f32[32,12,128]{2,0,1:T(8,128)} async-done(((f32[128,12,128]{2,0,1:T(8,128)}), f32[32,12,128]{2,0,1:T(8,128)}) %reduce-scatter.4.cloned.1.call-update) | async-done | bytes 196624 | tf_op jit(solution)/shard_map/reduce_scatter | solution.py:48
  117.2 0.0 copy-done
  117.2 0.0 copy-done.1
  117.2 1.2 multiply_multiply_fusion.1
  118.4 11.2 %all_gather.20 = f32[128,12,128]{2,0,1:T(8,128)S(1)} all-gather(f32[32,12,128]{2,0,1:T(8,128)S(1)} %get-tuple-element.5), channel_id=1, replica_groups=mesh['row'=4,'col'=8] {'row'}, dimensions={0}, use_global_device_ids=true | all-gather | bytes 983040 | tf_op jit(solution)/shard_map/all_gather | solution.py:46
  129.6 0.5 copy.24
  130.1 31.0 %all_to_all.54 = f32[128,12,128]{2,1,0:T(8,128)S(1)} all-to-all(f32[128,12,128]{2,1,0:T(8,128)S(1)} %copy.24), channel_id=1, replica_groups=mesh['row'=4,'col'=8] {'col'}, dimensions={0} | all-to-all | bytes 1572864 | tf_op jit(solution)/shard_map/all_to_all | solution.py:14
  161.0 0.2 copy.25
  161.3 0.7 constant_dynamic-slice_fusion.1
  162.0 0.0 all-gather.6.cloned.1.call-update
  162.0 0.0 reduce-scatter.6.cloned.1.call-start
  162.0 23.3 %all-gather.6.cloned.1.call-done = f32[128,24,128]{2,0,1:T(8,128)} async-done(((f32[16,24,128]{2,0,1:T(8,128)}), f32[128,24,128]{2,0,1:T(8,128)}) %all-gather.6.cloned.1.call-update) | async-done | bytes 1572880 | tf_op jit(solution)/shard_map/all_gather | solution.py:16
  185.4 14.3 %fusion.9 = f32[128,12,128]{2,0,1:T(8,128)} fusion(f32[24,12,128,128]{3,2,1,0:T(8,128)} %param.4, f32[128,24,128]{2,0,1:T(8,128)} %all-gather.6.cloned.1.call-done), kind=kOutput, calls=%fused_computation.7 | convolution fusion | flops 7247757312 | bytes 21233664 | tf_op jit(solution)/shard_map/isl,stlj->itj/dot_general | solution.py:20
  199.6 0.0 reduce-scatter.6.cloned.1.call-update
  199.6 0.0 all-gather.8.cloned.1.call-start
  199.7 25.4 %reduce-scatter.6.cloned.1.call-done = f32[32,12,128]{2,0,1:T(8,128)} async-done(((f32[128,12,128]{2,0,1:T(8,128)}), f32[32,12,128]{2,0,1:T(8,128)}) %reduce-scatter.6.cloned.1.call-update) | async-done | bytes 196624 | tf_op jit(solution)/shard_map/reduce_scatter | solution.py:48
  225.1 1.2 multiply_multiply_fusion
  226.3 11.2 %all_gather.22 = f32[128,12,128]{2,0,1:T(8,128)S(1)} all-gather(f32[32,12,128]{2,0,1:T(8,128)S(1)} %get-tuple-element.7), channel_id=1, replica_groups=mesh['row'=4,'col'=8] {'row'}, dimensions={0}, use_global_device_ids=true | all-gather | bytes 983040 | tf_op jit(solution)/shard_map/all_gather | solution.py:46
  237.5 0.5 copy.27
  238.0 31.0 %all_to_all.55 = f32[128,12,128]{2,1,0:T(8,128)S(1)} all-to-all(f32[128,12,128]{2,1,0:T(8,128)S(1)} %copy.27), channel_id=1, replica_groups=mesh['row'=4,'col'=8] {'col'}, dimensions={0} | all-to-all | bytes 1572864 | tf_op jit(solution)/shard_map/all_to_all | solution.py:14
  268.9 0.2 copy.28
  269.2 0.7 constant_dynamic-slice_fusion
  269.9 0.0 all-gather.8.cloned.1.call-update
  269.9 0.2 reduce-scatter.8.cloned.1.call-start
  270.1 23.1 %all-gather.8.cloned.1.call-done = f32[128,24,128]{2,0,1:T(8,128)} async-done(((f32[16,24,128]{2,0,1:T(8,128)}), f32[128,24,128]{2,0,1:T(8,128)}) %all-gather.8.cloned.1.call-update) | async-done | bytes 1572880 | tf_op jit(solution)/shard_map/all_gather | solution.py:16
  293.3 14.3 %fusion.12 = f32[128,12,128]{2,0,1:T(8,128)} fusion(f32[24,12,128,128]{3,2,1,0:T(8,128)} %param.4, f32[128,24,128]{2,0,1:T(8,128)} %all-gather.8.cloned.1.call-done), kind=kOutput, calls=%fused_computation.8 | convolution fusion | flops 7247757312 | bytes 21233664 | tf_op jit(solution)/shard_map/isl,stlj->itj/dot_general | solution.py:20
  307.5 0.0 reduce-scatter.8.cloned.1.call-update
  307.6 25.4 %reduce-scatter.8.cloned.1.call-done = f32[32,12,128]{2,0,1:T(8,128)} async-done(((f32[128,12,128]{2,0,1:T(8,128)}), f32[32,12,128]{2,0,1:T(8,128)}) %reduce-scatter.8.cloned.1.call-update) | async-done | bytes 196624 | tf_op jit(solution)/shard_map/reduce_scatter | solution.py:48
  333.0 1.2 fusion.17
  334.2 0.9 pad_maximum_fusion
Async XLA Ops:
  6.5 110.6 %copy-start = (f32[128,128]{1,0:T(8,128)S(1)}, f32[128,128]{1,0:T(8,128)}, u32[]{:S(2)}) copy-start(f32[128,128]{1,0:T(8,128)} %param.5) | copy-start | bytes 196612
  21.6 31.4 %all-to-all-start = ((f32[128,12,128]{2,1,0:T(8,128)}), f32[128,12,128]{2,1,0:T(8,128)S(1)}, u32[]{:S(2)}, u32[]{:S(2)}) async-start(f32[128,12,128]{2,1,0:T(8,128)} %copy.21), calls=%async_computation | async-start | bytes 2097152 | tf_op jit(solution)/shard_map/all_to_all | solution.py:14
  26.5 50.9 %all-gather.4.cloned.1.call-start = ((), (), s32[]{:S(2)}) async-start(), calls=%async_computation.6 | async-start | bytes 1769472 | tf_op jit(solution)/shard_map/all_gather | solution.py:16
  54.1 63.1 %copy-start.1 = (f32[32,12,128]{2,0,1:T(8,128)S(1)}, f32[32,12,128]{2,0,1:T(8,128)}, u32[]{:S(2)}) copy-start(f32[32,12,128]{2,0,1:T(8,128)} %param.3) | copy-start | bytes 589828
  54.1 63.1 %reduce-scatter.4.cloned.1.call-start = ((), (), s32[]{:S(2)}) async-start(), calls=%async_computation.7 | async-start | bytes 983040 | tf_op jit(solution)/shard_map/reduce_scatter | solution.py:48
  91.7 93.6 %all-gather.6.cloned.1.call-start = ((), (), s32[]{:S(2)}) async-start(), calls=%async_computation.8 | async-start | bytes 1769472 | tf_op jit(solution)/shard_map/all_gather | solution.py:16
  162.0 63.1 %reduce-scatter.6.cloned.1.call-start = ((), (), s32[]{:S(2)}) async-start(), calls=%async_computation.9 | async-start | bytes 983040 | tf_op jit(solution)/shard_map/reduce_scatter | solution.py:48
  199.6 93.6 %all-gather.8.cloned.1.call-start = ((), (), s32[]{:S(2)}) async-start(), calls=%async_computation.10 | async-start | bytes 1769472 | tf_op jit(solution)/shard_map/all_gather | solution.py:16
  269.9 63.1 %reduce-scatter.8.cloned.1.call-start = ((), (), s32[]{:S(2)}) async-start(), calls=%async_computation.11 | async-start | bytes 983040 | tf_op jit(solution)/shard_map/reduce_scatter | solution.py:48
Sparse Core Ops, SparseCore 0:
  54.2 23.2 all-gather.3
  91.9 25.2 reduce-scatter.3
  162.1 23.2 all-gather.5
  199.8 25.2 reduce-scatter.5
  270.0 23.2 all-gather.7
  307.7 25.2 reduce-scatter.7
where the time goes:
time: 342 us
  waiting for transfers between devices  173 us (51%)
  blocking collectives  96.9 us (28%)
  matrix products  46.5 us (14%)
  between operations  13.5 us (4%)
  starting transfers between devices  5.3 us (2%)
  local copies, waits for them, and re-layouts  5.23 us (2%)
    reduce_scatter x3, waiting for transfers between devices, per_device(): lax.psum_scatter(contract(sigma_rows, history), 'row', scatter_dimension=...  76.2 us
    all_gather x3, waiting for transfers between devices, sigma_panel(): return lax.all_gather(needed, 'col', axis=0, tiled=True)  69.8 us
    all_to_all x2, blocking collectives, sigma_panel(): lax.all_to_all(sigma_all, 'col', split_axis=0, concat_axis=1, tiled=True)  61.9 us
    dot_general x3, matrix products, contract(): jnp.einsum('isl,stlj->itj', sigma_rows, history, precision=lax.Precision....  42.8 us
    all_gather x3, blocking collectives, per_device(): sigma_all = lax.all_gather(sigma_local, 'row', axis=0, tiled=True)  35 us
    all_to_all x1, waiting for transfers between devices, sigma_panel(): lax.all_to_all(sigma_all, 'col', split_axis=0, concat_axis=1, tiled=True)  26.5 us
  transfers between devices with their start and end apart: 7, of which 7 were waited for; matrix products, arithmetic and copies ran while one was open for 0% of the time, Pallas kernels for 0%

commit v1 on v0

v1 whole, which is shorter than its diff:
```python
import functools

import jax
import jax.numpy as jnp
from jax import lax
from jax.experimental import pallas as pl
from jax.experimental.pallas import tpu as pltpu
from jax.sharding import PartitionSpec as P

STEPS = 3
CORES = 2

time_step = 0.2

AXES = ("row", "col")
VMEM = pltpu.VMEM


def split_kernel(slots, h_hbm, hi_ref, lo_ref, buf, sem):
    times, cols, depth, width = h_hbm.shape

    def copy(s):
        return pltpu.make_async_copy(h_hbm.at[s], buf.at[s % slots], sem.at[s % slots])

    for s in range(slots - 1):
        copy(s).start()

    def body(s, carry):
        @pl.when(s + slots - 1 < times)
        def _():
            copy(s + slots - 1).start()

        copy(s).wait()
        rows = pl.ds(pl.multiple_of(s * depth, depth), depth)
        for t in range(cols):
            tile = buf[s % slots, t]
            high = tile.astype(jnp.bfloat16)
            at = slice(t * width, (t + 1) * width)
            hi_ref[rows, at] = high
            lo_ref[rows, at] = (tile - high.astype(jnp.float32)).astype(jnp.bfloat16)
        return carry

    lax.fori_loop(0, times, body, 0)


def split_history(history):
    times, cols, depth, width = history.shape
    slots = 4
    shape = (times * depth, cols * width)
    return pl.pallas_call(
        functools.partial(split_kernel, slots),
        in_specs=[pl.BlockSpec(memory_space=pl.ANY)],
        out_specs=[pl.BlockSpec(memory_space=VMEM)] * 2,
        out_shape=[pltpu.VMEM(shape, jnp.bfloat16)] * 2,
        scratch_shapes=[
            pltpu.VMEM((slots, cols, depth, width), jnp.float32),
            pltpu.SemaphoreType.DMA((slots,)),
        ],
        compiler_params=pltpu.CompilerParams(vmem_limit_bytes=26 << 20),
        cost_estimate=pl.CostEstimate(
            flops=0, bytes_accessed=history.size * 8, transcendentals=0
        ),
        name="split_history",
    )(history)


def contract_kernel(panels, where, *refs):
    blocks = refs[:panels]
    hi_ref, lo_ref, out_ref, sig = refs[panels:]
    halves, cols, rows, depth = blocks[0].shape
    width = depth
    total = panels * rows
    for b in range(panels):
        for half in range(halves):
            at_half = where[panels + b] ^ half
            for t in range(cols):
                x = blocks[b][at_half, t]
                x = x * x * x
                high = x.astype(jnp.bfloat16)
                s = half * cols + t
                at = slice(s * depth, (s + 1) * depth)
                sig[b * rows : (b + 1) * rows, at] = high
                sig[total + b * rows : total + (b + 1) * rows, at] = (
                    x - high.astype(jnp.float32)
                ).astype(jnp.bfloat16)
    group = 4 if cols % 4 == 0 else 1
    for t0 in range(0, cols, group):
        at = slice(t0 * width, (t0 + group) * width)
        both = jnp.dot(sig[...], hi_ref[:, at], preferred_element_type=jnp.float32)
        rest = jnp.dot(
            sig[0:total, :], lo_ref[:, at], preferred_element_type=jnp.float32
        )
        value = both[0:total] + both[total:] + rest
        for b in range(panels):
            for t in range(group):
                out_ref[where[b], t0 + t] = value[
                    b * rows : (b + 1) * rows, t * width : (t + 1) * width
                ]


def contract(where, blocks, hi, lo):
    panels = len(blocks)
    halves, cols, rows, depth = blocks[0].shape
    inner, outer = hi.shape
    total = panels * rows
    return pl.pallas_call(
        functools.partial(contract_kernel, panels),
        in_specs=[pl.BlockSpec(memory_space=pltpu.SMEM)]
        + [pl.BlockSpec(memory_space=VMEM)] * (panels + 2),
        out_specs=pl.BlockSpec(memory_space=VMEM),
        out_shape=jax.ShapeDtypeStruct(
            (panels, outer // depth, rows, depth), jnp.float32
        ),
        scratch_shapes=[pltpu.VMEM((2 * total, inner), jnp.bfloat16)],
        compiler_params=pltpu.CompilerParams(vmem_limit_bytes=12 << 20),
        cost_estimate=pl.CostEstimate(
            flops=6 * total * inner * outer, bytes_accessed=4 << 20, transcendentals=0
        ),
        name="contract",
    )(where, *blocks, hi, lo)


def pairs(nrow, ncol, target):
    listed = []
    for r in range(nrow):
        for c in range(ncol):
            to_r, to_c = target(r, c // CORES, c % CORES)
            listed.append((r * ncol + c, to_r * ncol + to_c))
    return listed


def per_device(nrow, ncol, new_row, history, hamiltonian):
    def move(value, target):
        return lax.ppermute(value, AXES, pairs(nrow, ncol, target))

    def partner(value):
        return move(value, lambda r, m, k: (r, m * CORES + 1 - k))

    r = lax.axis_index("row")
    m, k = lax.axis_index("col") // CORES, lax.axis_index("col") % CORES
    turns = [(d, nrow - 1 - d) for d in range(nrow // CORES)]
    sends = [
        lambda r, m, k, turn=turn: (m, (r ^ turn[k]) * CORES + k) for turn in turns
    ]
    own = [jnp.where(k == 0, turn[0], turn[1]) for turn in turns]
    theirs = [jnp.where(k == 0, turn[1], turn[0]) for turn in turns]
    where = jnp.stack(
        [m ^ d ^ r for d in own + theirs]
        + [k for _ in own]
        + [1 - k for _ in theirs]
    ).astype(jnp.int32)

    hi, lo = split_history(history)
    current = jnp.transpose(new_row, (1, 0, 2))
    results = []
    for step_index in range(STEPS):
        both = jnp.stack([current, partner(current)])
        mine = [move(both, send) for send in sends]
        other = [partner(block) for block in mine]
        parts = contract(where, mine + other, hi, lo)
        kinetic = jnp.einsum(
            "til,lj->tij",
            current,
            hamiltonian,
            precision=lax.Precision.HIGHEST,
            preferred_element_type=jnp.float32,
        )
        collision = parts[0]
        for x in range(1, nrow):
            collision = collision + move(
                parts[x], lambda r, m, k, x=x: (r ^ x, m * CORES + k)
            )
        current = current - time_step * (kinetic + collision)
        results.append(jnp.transpose(current, (1, 0, 2)))
    return jnp.stack(results)


def solution(mesh):
    placed = (P("row", "col", None), P("row", "col", None, None), P())
    return jax.shard_map(
        functools.partial(per_device, mesh.shape["row"], mesh.shape["col"]),
        mesh=mesh,
        in_specs=placed,
        out_specs=P(None, "row", "col", None),
        check_vma=False,
    )
```

time: 342 us -> 155 us (0.45)
  waiting for transfers between devices: 173 us -> 64.7 us
  blocking collectives: 96.9 us -> 0 us
  matrix products: 46.5 us -> 0.95 us
  starting transfers between devices: 5.3 us -> 50.1 us
  Pallas kernels: 0 us -> 22.4 us
  between operations: 13.5 us -> 0.2 us
  local copies, waits for them, and re-layouts: 5.23 us -> 14.8 us
    reduce_scatter x3 -> x0, waiting for transfers between devices: 76.2 us -> none  [per_device(): lax.psum_scatter(contract(sigma_rows, history), 'row', scatter_dimension=...]
    all_gather x3 -> x0, waiting for transfers between devices: 69.8 us -> none  [sigma_panel(): return lax.all_gather(needed, 'col', axis=0, tiled=True)]
    ppermute x0 -> x24, waiting for transfers between devices: none -> 64.7 us  [move(): return lax.ppermute(value, AXES, pairs(nrow, ncol, target))]
    all_to_all x2 -> x0, blocking collectives: 61.9 us -> none  [sigma_panel(): lax.all_to_all(sigma_all, 'col', split_axis=0, concat_axis=1, tiled=True)]
    ppermute x0 -> x24, starting transfers between devices: none -> 50.1 us  [move(): return lax.ppermute(value, AXES, pairs(nrow, ncol, target))]
    dot_general x6 -> x3, matrix products: 46.5 us -> 0.95 us  [per_device(): jnp.einsum('til,lj->tij', current, hamiltonian, precision=lax.Precision.H...]
    all_gather x3 -> x0, blocking collectives: 35 us -> none  [per_device(): sigma_all = lax.all_gather(sigma_local, 'row', axis=0, tiled=True)]
    all_to_all x1 -> x0, waiting for transfers between devices: 26.5 us -> none  [sigma_panel(): lax.all_to_all(sigma_all, 'col', split_axis=0, concat_axis=1, tiled=True)]
  transfers between devices with their start and end apart: 7 -> 24, of which waited for: 7 -> 15; matrix products, arithmetic and copies ran while one was open for 0% -> 0% of each run, Pallas kernels for 0% -> 6%
where the time goes in v1:
time: 155 us
  waiting for transfers between devices  64.7 us (42%)
  starting transfers between devices  50.1 us (32%)
  Pallas kernels  22.4 us (14%)
  local copies, waits for them, and re-layouts  14.8 us (10%)
  other arithmetic  1.97 us (1%)
    ppermute x24, waiting for transfers between devices, move(): return lax.ppermute(value, AXES, pairs(nrow, ncol, target))  64.7 us
    ppermute x24, starting transfers between devices, move(): return lax.ppermute(value, AXES, pairs(nrow, ncol, target))  50.1 us
    unnamed x14, local copies, waits for them, and re-layouts  14.6 us
    pallas_call x3, Pallas kernels, contract(): pl.pallas_call(functools.partial(contract_kernel, panels), in_specs=[pl.B...  13.3 us
    pallas_call x1, Pallas kernels, split_history(): pl.pallas_call(functools.partial(split_kernel, slots), in_specs=[pl.Block...  9.08 us
  transfers between devices with their start and end apart: 24, of which 15 were waited for; matrix products, arithmetic and copies ran while one was open for 0% of the time, Pallas kernels for 6%

profile of v1, /device:TPU:0, one launch (start us, length us, event | category | flops | bytes accessed | tf_op | source)
XLA Modules:
  0.0 155.1 jit_solution(17633255117321346992)
XLA Ops:
  0.0 0.5 collective-permute-start
  0.5 1.3 collective-permute-done
  1.8 1.0 pad_maximum_fusion.1
  2.7 3.0 %collective-permute-start.2 = (f32[2,12,32,128]{3,2,1,0:T(8,128)S(1)}, f32[2,12,32,128]{3,2,1,0:T(8,128)S(1)}, u32[]{:S(2)}, u32[]{:S(2)}) collective-permute-start(f32[2,12,32,128]{3,2,1,0:T(8,128)S(1)} %pad_maximum_fusion.1), channel_id=1, source_target_pairs={{0,2},{1,5},{2,10},{3,13},{4,18},{5,21},{6,26},{7,29},{8,0},{9,7},... | collective-permute-start | bytes 1179656 | tf_op jit(solution)/shard_map/ppermute | solution.py:134
  5.7 0.7 collective-permute-start.1
  6.4 8.6 %collective-permute-done.2.refs_1_ = f32[2,12,32,128]{3,2,1,0:T(8,128)S(1)} collective-permute-done((f32[2,12,32,128]{3,2,1,0:T(8,128)S(1)}, f32[2,12,32,128]{3,2,1,0:T(8,128)S(1)}, u32[]{:S(2)}, u32[]{:S(2)}) %collective-permute-start.2) | collective-permute-done | bytes 393248 | tf_op jit(solution)/shard_map/ppermute | solution.py:134
  15.0 0.3 collective-permute-start.4
  15.4 4.2 %collective-permute-start.3 = (f32[2,12,32,128]{3,2,1,0:T(8,128)S(1)}, f32[2,12,32,128]{3,2,1,0:T(8,128)S(1)}, u32[]{:S(2)}, u32[]{:S(2)}) collective-permute-start(f32[2,12,32,128]{3,2,1,0:T(8,128)S(1)} %collective-permute-done.1.refs_0_), channel_id=1, source_target_pairs={{0,1},{1,0},{2,3},{3,2},{4,5},{5,4},{6,7},{7,6},{8,9},{9,8},{10,11... | collective-permute-start | bytes 1179656 | tf_op jit(solution)/shard_map/ppermute | solution.py:134
  19.6 9.1 %split_history.1 = (bf16[3072,1536]{1,0:T(8,128)(2,1)S(1)}, bf16[3072,1536]{1,0:T(8,128)(2,1)S(1)}) custom-call(f32[24,12,128,128]{3,2,1,0:T(8,128)} %h_hbm.1), custom_call_target="tpu_custom_call" | custom-call | bytes 37748736 | tf_op jit(solution)/shard_map/split_history/pallas_call | solution.py:50
  28.7 3.6 %copy-done.1 = bf16[3072,1536]{1,0:T(8,128)(2,1)} copy-done((bf16[3072,1536]{1,0:T(8,128)(2,1)}, bf16[3072,1536]{1,0:T(8,128)(2,1)S(1)}, u32[]{:S(2)}) %copy-start.1) | copy-done | bytes 9437208
  32.3 3.6 %copy-done.4 = bf16[3072,1536]{1,0:T(8,128)(2,1)} copy-done((bf16[3072,1536]{1,0:T(8,128)(2,1)}, bf16[3072,1536]{1,0:T(8,128)(2,1)S(1)}, u32[]{:S(2)}) %copy-start.4) | copy-done | bytes 9437208
  36.0 0.1 stack.68.where
  36.1 3.7 %copy-done.2 = bf16[3072,1536]{1,0:T(8,128)(2,1)S(1)} copy-done((bf16[3072,1536]{1,0:T(8,128)(2,1)S(1)}, bf16[3072,1536]{1,0:T(8,128)(2,1)}, u32[]{:S(2)}) %copy-start.2) | copy-done | bytes 9437208
  39.7 3.7 %copy-done.5 = bf16[3072,1536]{1,0:T(8,128)(2,1)S(1)} copy-done((bf16[3072,1536]{1,0:T(8,128)(2,1)S(1)}, bf16[3072,1536]{1,0:T(8,128)(2,1)}, u32[]{:S(2)}) %copy-start.5) | copy-done | bytes 9437208
  43.4 4.4 %contract.3 = f32[4,12,32,128]{3,2,1,0:T(8,128)S(1)} custom-call(s32[8]{0:T(128)S(1)} %stack.68.where, f32[2,12,32,128]{3,2,1,0:T(8,128)S(1)} %collective-permute-done.1.refs_0_, f32[2,12,32,128]{3,2,1,0:T(8,128)S(1)} %collective-permute-done.2.refs_1_, f32[2,12,32,128]{3,2,1,0:T(8,128)S(1)} %collective-permute-done.3.refs_2_, ...), custom_call_target="tpu_custom_call" | custom-call | flops 3623878656 | bytes 4194304 | tf_op jit(solution)/shard_map/contract/pallas_call | solution.py:106
  47.8 3.1 %collective-permute-start.5 = (f32[12,32,128]{2,1,0:T(8,128)S(1)}, f32[12,32,128]{2,1,0:T(8,128)S(1)}, u32[]{:S(2)}, u32[]{:S(2)}) collective-permute-start(f32[12,32,128]{2,1,0:T(8,128)S(1)} %get-tuple-element.15), channel_id=1, source_target_pairs={{0,8},{1,9},{2,10},{3,11},{4,12},{5,13},{6,14},{7,15},{8,0},{9,1},... | collective-permute-start | bytes 589832 | tf_op jit(solution)/shard_map/ppermute | solution.py:134
  50.9 6.8 %collective-permute-start.7 = (f32[12,32,128]{2,1,0:T(8,128)S(1)}, f32[12,32,128]{2,1,0:T(8,128)S(1)}, u32[]{:S(2)}, u32[]{:S(2)}) collective-permute-start(f32[12,32,128]{2,1,0:T(8,128)S(1)} %get-tuple-element.16), channel_id=1, source_target_pairs={{0,24},{1,25},{2,26},{3,27},{4,28},{5,29},{6,30},{7,31},{8,16},{9,... | collective-permute-start | bytes 589832 | tf_op jit(solution)/shard_map/ppermute | solution.py:134
  57.8 0.3 fusion.19
  58.1 9.3 %collective-permute-done.7 = f32[12,32,128]{2,1,0:T(8,128)S(1)} collective-permute-done((f32[12,32,128]{2,1,0:T(8,128)S(1)}, f32[12,32,128]{2,1,0:T(8,128)S(1)}, u32[]{:S(2)}, u32[]{:S(2)}) %collective-permute-start.7) | collective-permute-done | bytes 196640 | tf_op jit(solution)/shard_map/ppermute | solution.py:134
  67.4 1.4 collective-permute-done.6
  68.7 0.1 fusion.16
  68.9 1.4 collective-permute-done.8
  70.4 1.4 collective-permute-start.10
  71.8 0.7 collective-permute-start.9
  72.5 8.8 %collective-permute-done.10.refs_1_ = f32[2,12,32,128]{3,2,1,0:T(8,128)S(1)} collective-permute-done((f32[2,12,32,128]{3,2,1,0:T(8,128)S(1)}, f32[2,12,32,128]{3,2,1,0:T(8,128)S(1)}, u32[]{:S(2)}, u32[]{:S(2)}) %collective-permute-start.10) | collective-permute-done | bytes 393248 | tf_op jit(solution)/shard_map/ppermute | solution.py:134
  81.3 0.3 collective-permute-start.12
  81.5 4.2 %collective-permute-start.11 = (f32[2,12,32,128]{3,2,1,0:T(8,128)S(1)}, f32[2,12,32,128]{3,2,1,0:T(8,128)S(1)}, u32[]{:S(2)}, u32[]{:S(2)}) collective-permute-start(f32[2,12,32,128]{3,2,1,0:T(8,128)S(1)} %collective-permute-done.9.refs_0_), channel_id=1, source_target_pairs={{0,1},{1,0},{2,3},{3,2},{4,5},{5,4},{6,7},{7,6},{8,9},{9,8},{10,11... | collective-permute-start | bytes 1179656 | tf_op jit(solution)/shard_map/ppermute | solution.py:134
  85.7 1.3 collective-permute-done.11.refs_2_
  87.1 4.5 %contract.4 = f32[4,12,32,128]{3,2,1,0:T(8,128)S(1)} custom-call(s32[8]{0:T(128)S(1)} %stack.68.where, f32[2,12,32,128]{3,2,1,0:T(8,128)S(1)} %collective-permute-done.9.refs_0_, f32[2,12,32,128]{3,2,1,0:T(8,128)S(1)} %collective-permute-done.10.refs_1_, f32[2,12,32,128]{3,2,1,0:T(8,128)S(1)} %collective-permute-done.11.refs_2_, ...), custom_call_target="tpu_custom_call" | custom-call | flops 3623878656 | bytes 4194304 | tf_op jit(solution)/shard_map/contract/pallas_call | solution.py:106
  91.6 1.9 %collective-permute-start.13 = (f32[12,32,128]{2,1,0:T(8,128)S(1)}, f32[12,32,128]{2,1,0:T(8,128)S(1)}, u32[]{:S(2)}, u32[]{:S(2)}) collective-permute-start(f32[12,32,128]{2,1,0:T(8,128)S(1)} %get-tuple-element.12), channel_id=1, source_target_pairs={{0,8},{1,9},{2,10},{3,11},{4,12},{5,13},{6,14},{7,15},{8,0},{9,1},... | collective-permute-start | bytes 589832 | tf_op jit(solution)/shard_map/ppermute | solution.py:134
  93.5 7.1 %collective-permute-start.15 = (f32[12,32,128]{2,1,0:T(8,128)S(1)}, f32[12,32,128]{2,1,0:T(8,128)S(1)}, u32[]{:S(2)}, u32[]{:S(2)}) collective-permute-start(f32[12,32,128]{2,1,0:T(8,128)S(1)} %get-tuple-element.13), channel_id=1, source_target_pairs={{0,24},{1,25},{2,26},{3,27},{4,28},{5,29},{6,30},{7,31},{8,16},{9,... | collective-permute-start | bytes 589832 | tf_op jit(solution)/shard_map/ppermute | solution.py:134
  100.5 9.2 %collective-permute-done.15 = f32[12,32,128]{2,1,0:T(8,128)S(1)} collective-permute-done((f32[12,32,128]{2,1,0:T(8,128)S(1)}, f32[12,32,128]{2,1,0:T(8,128)S(1)}, u32[]{:S(2)}, u32[]{:S(2)}) %collective-permute-start.15) | collective-permute-done | bytes 196640 | tf_op jit(solution)/shard_map/ppermute | solution.py:134
  109.8 1.4 collective-permute-done.14
  111.1 0.3 fusion.4
  111.5 1.4 collective-permute-done.16
  113.0 1.5 collective-permute-start.18
  114.5 0.9 collective-permute-start.17
  115.4 8.7 %collective-permute-done.18.refs_1_ = f32[2,12,32,128]{3,2,1,0:T(8,128)S(1)} collective-permute-done((f32[2,12,32,128]{3,2,1,0:T(8,128)S(1)}, f32[2,12,32,128]{3,2,1,0:T(8,128)S(1)}, u32[]{:S(2)}, u32[]{:S(2)}) %collective-permute-start.18) | collective-permute-done | bytes 393248 | tf_op jit(solution)/shard_map/ppermute | solution.py:134
  124.1 3.4 %collective-permute-start.19 = (f32[2,12,32,128]{3,2,1,0:T(8,128)S(1)}, f32[2,12,32,128]{3,2,1,0:T(8,128)S(1)}, u32[]{:S(2)}, u32[]{:S(2)}) collective-permute-start(f32[2,12,32,128]{3,2,1,0:T(8,128)S(1)} %collective-permute-done.17.refs_0_), channel_id=1, source_target_pairs={{0,1},{1,0},{2,3},{3,2},{4,5},{5,4},{6,7},{7,6},{8,9},{9,8},{10,11... | collective-permute-start | bytes 1179656 | tf_op jit(solution)/shard_map/ppermute | solution.py:134
  127.4 1.3 collective-permute-done.19.refs_2_
  128.8 4.5 %contract.5 = f32[4,12,32,128]{3,2,1,0:T(8,128)S(1)} custom-call(s32[8]{0:T(128)S(1)} %stack.68.where, f32[2,12,32,128]{3,2,1,0:T(8,128)S(1)} %collective-permute-done.17.refs_0_, f32[2,12,32,128]{3,2,1,0:T(8,128)S(1)} %collective-permute-done.18.refs_1_, f32[2,12,32,128]{3,2,1,0:T(8,128)S(1)} %collective-permute-done.19.refs_2_, ...), custom_call_target="tpu_custom_call" | custom-call | flops 3623878656 | bytes 4194304 | tf_op jit(solution)/shard_map/contract/pallas_call | solution.py:106
  133.3 7.9 %collective-permute-start.21 = (f32[12,32,128]{2,1,0:T(8,128)S(1)}, f32[12,32,128]{2,1,0:T(8,128)S(1)}, u32[]{:S(2)}, u32[]{:S(2)}) collective-permute-start(f32[12,32,128]{2,1,0:T(8,128)S(1)} %get-tuple-element.9), channel_id=1, source_target_pairs={{0,8},{1,9},{2,10},{3,11},{4,12},{5,13},{6,14},{7,15},{8,0},{9,1},... | collective-permute-start | bytes 589832 | tf_op jit(solution)/shard_map/ppermute | solution.py:134
  141.2 2.1 %collective-permute-start.23 = (f32[12,32,128]{2,1,0:T(8,128)S(1)}, f32[12,32,128]{2,1,0:T(8,128)S(1)}, u32[]{:S(2)}, u32[]{:S(2)}) collective-permute-start(f32[12,32,128]{2,1,0:T(8,128)S(1)} %get-tuple-element.10), channel_id=1, source_target_pairs={{0,24},{1,25},{2,26},{3,27},{4,28},{5,29},{6,30},{7,31},{8,16},{9,... | collective-permute-start | bytes 589832 | tf_op jit(solution)/shard_map/ppermute | solution.py:134
  143.3 3.7 %collective-permute-done.21 = f32[12,32,128]{2,1,0:T(8,128)S(1)} collective-permute-done((f32[12,32,128]{2,1,0:T(8,128)S(1)}, f32[12,32,128]{2,1,0:T(8,128)S(1)}, u32[]{:S(2)}, u32[]{:S(2)}) %collective-permute-start.21) | collective-permute-done | bytes 196640 | tf_op jit(solution)/shard_map/ppermute | solution.py:134
  147.0 5.6 %collective-permute-done.23 = f32[12,32,128]{2,1,0:T(8,128)S(1)} collective-permute-done((f32[12,32,128]{2,1,0:T(8,128)S(1)}, f32[12,32,128]{2,1,0:T(8,128)S(1)}, u32[]{:S(2)}, u32[]{:S(2)}) %collective-permute-start.23) | collective-permute-done | bytes 196640 | tf_op jit(solution)/shard_map/ppermute | solution.py:134
  152.6 1.4 collective-permute-done.22
  153.9 0.3 fusion.2
  154.3 0.9 pad_maximum_fusion
  (30 shorter events, 0.4 us)
Async XLA Ops:
  0.0 57.8 %copy-start = (f32[128,128]{1,0:T(8,128)S(1)}, f32[128,128]{1,0:T(8,128)}, u32[]{:S(2)}) copy-start(f32[128,128]{1,0:T(8,128)} %param.5) | copy-start | bytes 196612
  0.0 1.8 %collective-permute-start = (f32[12,32,128]{2,1,0:T(8,128)}, f32[12,32,128]{2,1,0:T(8,128)S(1)}, u32[]{:S(2)}, u32[]{:S(2)}) collective-permute-start(f32[12,32,128]{2,1,0:T(8,128)} %bitcast.92), channel_id=1, source_target_pairs={{0,1},{1,0},{2,3},{3,2},{4,5},{5,4},{6,7},{7,6},{8,9},{9,8},{10,11... | collective-permute-start | bytes 589832 | tf_op jit(solution)/shard_map/ppermute | solution.py:134
  2.7 12.3 %collective-permute-start.2 = (f32[2,12,32,128]{3,2,1,0:T(8,128)S(1)}, f32[2,12,32,128]{3,2,1,0:T(8,128)S(1)}, u32[]{:S(2)}, u32[]{:S(2)}) collective-permute-start(f32[2,12,32,128]{3,2,1,0:T(8,128)S(1)} %pad_maximum_fusion.1), channel_id=1, source_target_pairs={{0,2},{1,5},{2,10},{3,13},{4,18},{5,21},{6,26},{7,29},{8,0},{9,7},... | collective-permute-start | bytes 1179656 | tf_op jit(solution)/shard_map/ppermute | solution.py:134
  5.7 9.7 %collective-permute-start.1 = (f32[2,12,32,128]{3,2,1,0:T(8,128)S(1)}, f32[2,12,32,128]{3,2,1,0:T(8,128)S(1)}, u32[]{:S(2)}, u32[]{:S(2)}) collective-permute-start(f32[2,12,32,128]{3,2,1,0:T(8,128)S(1)} %pad_maximum_fusion.1), channel_id=1, source_target_pairs={{0,0},{1,7},{2,8},{3,15},{4,16},{5,23},{6,24},{7,31},{8,2},{9,5},{... | collective-permute-start | bytes 1179656 | tf_op jit(solution)/shard_map/ppermute | solution.py:134
  15.0 21.0 %collective-permute-start.4 = (f32[2,12,32,128]{3,2,1,0:T(8,128)S(1)}, f32[2,12,32,128]{3,2,1,0:T(8,128)S(1)}, u32[]{:S(2)}, u32[]{:S(2)}) collective-permute-start(f32[2,12,32,128]{3,2,1,0:T(8,128)S(1)} %collective-permute-done.2.refs_1_), channel_id=1, source_target_pairs={{0,1},{1,0},{2,3},{3,2},{4,5},{5,4},{6,7},{7,6},{8,9},{9,8},{10,11... | collective-permute-start | bytes 1179656 | tf_op jit(solution)/shard_map/ppermute | solution.py:134
  15.4 20.7 %collective-permute-start.3 = (f32[2,12,32,128]{3,2,1,0:T(8,128)S(1)}, f32[2,12,32,128]{3,2,1,0:T(8,128)S(1)}, u32[]{:S(2)}, u32[]{:S(2)}) collective-permute-start(f32[2,12,32,128]{3,2,1,0:T(8,128)S(1)} %collective-permute-done.1.refs_0_), channel_id=1, source_target_pairs={{0,1},{1,0},{2,3},{3,2},{4,5},{5,4},{6,7},{7,6},{8,9},{9,8},{10,11... | collective-permute-start | bytes 1179656 | tf_op jit(solution)/shard_map/ppermute | solution.py:134
  28.7 3.7 %copy-start.1 = (bf16[3072,1536]{1,0:T(8,128)(2,1)}, bf16[3072,1536]{1,0:T(8,128)(2,1)S(1)}, u32[]{:S(2)}) copy-start(bf16[3072,1536]{1,0:T(8,128)(2,1)S(1)} %get-tuple-element.7.refs_4_) | copy-start | bytes 28311556
  32.3 3.6 %copy-start.4 = (bf16[3072,1536]{1,0:T(8,128)(2,1)}, bf16[3072,1536]{1,0:T(8,128)(2,1)S(1)}, u32[]{:S(2)}) copy-start(bf16[3072,1536]{1,0:T(8,128)(2,1)S(1)} %get-tuple-element.8.refs_5_) | copy-start | bytes 28311556
  36.0 3.7 %copy-start.2 = (bf16[3072,1536]{1,0:T(8,128)(2,1)S(1)}, bf16[3072,1536]{1,0:T(8,128)(2,1)}, u32[]{:S(2)}) copy-start(bf16[3072,1536]{1,0:T(8,128)(2,1)} %copy-done.1) | copy-start | bytes 28311556
  39.7 3.7 %copy-start.5 = (bf16[3072,1536]{1,0:T(8,128)(2,1)S(1)}, bf16[3072,1536]{1,0:T(8,128)(2,1)}, u32[]{:S(2)}) copy-start(bf16[3072,1536]{1,0:T(8,128)(2,1)} %copy-done.4) | copy-start | bytes 28311556
  43.4 14.3 %copy-start.6 = (f32[32,12,128]{2,0,1:T(8,128)S(1)}, f32[32,12,128]{2,0,1:T(8,128)}, u32[]{:S(2)}) copy-start(f32[32,12,128]{2,0,1:T(8,128)} %param.3) | copy-start | bytes 589828
  43.4 43.6 %copy-start.3 = (bf16[3072,1536]{1,0:T(8,128)(2,1)S(1)}, bf16[3072,1536]{1,0:T(8,128)(2,1)}, u32[]{:S(2)}) copy-start(bf16[3072,1536]{1,0:T(8,128)(2,1)} %copy-done.1) | copy-start | bytes 28311556
  47.8 10.2 %collective-permute-start.5 = (f32[12,32,128]{2,1,0:T(8,128)S(1)}, f32[12,32,128]{2,1,0:T(8,128)S(1)}, u32[]{:S(2)}, u32[]{:S(2)}) collective-permute-start(f32[12,32,128]{2,1,0:T(8,128)S(1)} %get-tuple-element.15), channel_id=1, source_target_pairs={{0,8},{1,9},{2,10},{3,11},{4,12},{5,13},{6,14},{7,15},{8,0},{9,1},... | collective-permute-start | bytes 589832 | tf_op jit(solution)/shard_map/ppermute | solution.py:134
  50.9 16.4 %collective-permute-start.7 = (f32[12,32,128]{2,1,0:T(8,128)S(1)}, f32[12,32,128]{2,1,0:T(8,128)S(1)}, u32[]{:S(2)}, u32[]{:S(2)}) collective-permute-start(f32[12,32,128]{2,1,0:T(8,128)S(1)} %get-tuple-element.16), channel_id=1, source_target_pairs={{0,24},{1,25},{2,26},{3,27},{4,28},{5,29},{6,30},{7,31},{8,16},{9,... | collective-permute-start | bytes 589832 | tf_op jit(solution)/shard_map/ppermute | solution.py:134
  57.8 11.0 %collective-permute-start.6 = (f32[12,32,128]{2,1,0:T(8,128)S(1)}, f32[12,32,128]{2,1,0:T(8,128)S(1)}, u32[]{:S(2)}, u32[]{:S(2)}) collective-permute-start(f32[12,32,128]{2,1,0:T(8,128)S(1)} %get-tuple-element.17), channel_id=1, source_target_pairs={{0,16},{1,17},{2,18},{3,19},{4,20},{5,21},{6,22},{7,23},{8,24},{9,... | collective-permute-start | bytes 589832 | tf_op jit(solution)/shard_map/ppermute | solution.py:134
  68.8 1.5 collective-permute-start.8
  70.4 10.9 %collective-permute-start.10 = (f32[2,12,32,128]{3,2,1,0:T(8,128)S(1)}, f32[2,12,32,128]{3,2,1,0:T(8,128)S(1)}, u32[]{:S(2)}, u32[]{:S(2)}) collective-permute-start(f32[2,12,32,128]{3,2,1,0:T(8,128)S(1)} %pad_maximum_fusion.2), channel_id=1, source_target_pairs={{0,2},{1,5},{2,10},{3,13},{4,18},{5,21},{6,26},{7,29},{8,0},{9,7},... | collective-permute-start | bytes 1179656 | tf_op jit(solution)/shard_map/ppermute | solution.py:134
  71.8 9.7 %collective-permute-start.9 = (f32[2,12,32,128]{3,2,1,0:T(8,128)S(1)}, f32[2,12,32,128]{3,2,1,0:T(8,128)S(1)}, u32[]{:S(2)}, u32[]{:S(2)}) collective-permute-start(f32[2,12,32,128]{3,2,1,0:T(8,128)S(1)} %pad_maximum_fusion.2), channel_id=1, source_target_pairs={{0,0},{1,7},{2,8},{3,15},{4,16},{5,23},{6,24},{7,31},{8,2},{9,5},{... | collective-permute-start | bytes 1179656 | tf_op jit(solution)/shard_map/ppermute | solution.py:134
  81.3 4.5 %collective-permute-start.12 = (f32[2,12,32,128]{3,2,1,0:T(8,128)S(1)}, f32[2,12,32,128]{3,2,1,0:T(8,128)S(1)}, u32[]{:S(2)}, u32[]{:S(2)}) collective-permute-start(f32[2,12,32,128]{3,2,1,0:T(8,128)S(1)} %collective-permute-done.10.refs_1_), channel_id=1, source_target_pairs={{0,1},{1,0},{2,3},{3,2},{4,5},{5,4},{6,7},{7,6},{8,9},{9,8},{10,11... | collective-permute-start | bytes 1179656 | tf_op jit(solution)/shard_map/ppermute | solution.py:134
  81.5 5.5 %collective-permute-start.11 = (f32[2,12,32,128]{3,2,1,0:T(8,128)S(1)}, f32[2,12,32,128]{3,2,1,0:T(8,128)S(1)}, u32[]{:S(2)}, u32[]{:S(2)}) collective-permute-start(f32[2,12,32,128]{3,2,1,0:T(8,128)S(1)} %collective-permute-done.9.refs_0_), channel_id=1, source_target_pairs={{0,1},{1,0},{2,3},{3,2},{4,5},{5,4},{6,7},{7,6},{8,9},{9,8},{10,11... | collective-permute-start | bytes 1179656 | tf_op jit(solution)/shard_map/ppermute | solution.py:134
  91.6 9.0 %collective-permute-start.13 = (f32[12,32,128]{2,1,0:T(8,128)S(1)}, f32[12,32,128]{2,1,0:T(8,128)S(1)}, u32[]{:S(2)}, u32[]{:S(2)}) collective-permute-start(f32[12,32,128]{2,1,0:T(8,128)S(1)} %get-tuple-element.12), channel_id=1, source_target_pairs={{0,8},{1,9},{2,10},{3,11},{4,12},{5,13},{6,14},{7,15},{8,0},{9,1},... | collective-permute-start | bytes 589832 | tf_op jit(solution)/shard_map/ppermute | solution.py:134
  93.5 16.3 %collective-permute-start.15 = (f32[12,32,128]{2,1,0:T(8,128)S(1)}, f32[12,32,128]{2,1,0:T(8,128)S(1)}, u32[]{:S(2)}, u32[]{:S(2)}) collective-permute-start(f32[12,32,128]{2,1,0:T(8,128)S(1)} %get-tuple-element.13), channel_id=1, source_target_pairs={{0,24},{1,25},{2,26},{3,27},{4,28},{5,29},{6,30},{7,31},{8,16},{9,... | collective-permute-start | bytes 589832 | tf_op jit(solution)/shard_map/ppermute | solution.py:134
  100.5 10.6 %collective-permute-start.14 = (f32[12,32,128]{2,1,0:T(8,128)S(1)}, f32[12,32,128]{2,1,0:T(8,128)S(1)}, u32[]{:S(2)}, u32[]{:S(2)}) collective-permute-start(f32[12,32,128]{2,1,0:T(8,128)S(1)} %get-tuple-element.14), channel_id=1, source_target_pairs={{0,16},{1,17},{2,18},{3,19},{4,20},{5,21},{6,22},{7,23},{8,24},{9,... | collective-permute-start | bytes 589832 | tf_op jit(solution)/shard_map/ppermute | solution.py:134
  111.5 1.5 collective-permute-start.16
  113.0 11.0 %collective-permute-start.18 = (f32[2,12,32,128]{3,2,1,0:T(8,128)S(1)}, f32[2,12,32,128]{3,2,1,0:T(8,128)S(1)}, u32[]{:S(2)}, u32[]{:S(2)}) collective-permute-start(f32[2,12,32,128]{3,2,1,0:T(8,128)S(1)} %pad_maximum_fusion.3), channel_id=1, source_target_pairs={{0,2},{1,5},{2,10},{3,13},{4,18},{5,21},{6,26},{7,29},{8,0},{9,7},... | collective-permute-start | bytes 1179656 | tf_op jit(solution)/shard_map/ppermute | solution.py:134
  114.5 9.5 %collective-permute-start.17 = (f32[2,12,32,128]{3,2,1,0:T(8,128)S(1)}, f32[2,12,32,128]{3,2,1,0:T(8,128)S(1)}, u32[]{:S(2)}, u32[]{:S(2)}) collective-permute-start(f32[2,12,32,128]{3,2,1,0:T(8,128)S(1)} %pad_maximum_fusion.3), channel_id=1, source_target_pairs={{0,0},{1,7},{2,8},{3,15},{4,16},{5,23},{6,24},{7,31},{8,2},{9,5},{... | collective-permute-start | bytes 1179656 | tf_op jit(solution)/shard_map/ppermute | solution.py:134
  124.1 3.4 %collective-permute-start.20 = (f32[2,12,32,128]{3,2,1,0:T(8,128)S(1)}, f32[2,12,32,128]{3,2,1,0:T(8,128)S(1)}, u32[]{:S(2)}, u32[]{:S(2)}) collective-permute-start(f32[2,12,32,128]{3,2,1,0:T(8,128)S(1)} %collective-permute-done.18.refs_1_), channel_id=1, source_target_pairs={{0,1},{1,0},{2,3},{3,2},{4,5},{5,4},{6,7},{7,6},{8,9},{9,8},{10,11... | collective-permute-start | bytes 1179656 | tf_op jit(solution)/shard_map/ppermute | solution.py:134
  124.1 4.7 %collective-permute-start.19 = (f32[2,12,32,128]{3,2,1,0:T(8,128)S(1)}, f32[2,12,32,128]{3,2,1,0:T(8,128)S(1)}, u32[]{:S(2)}, u32[]{:S(2)}) collective-permute-start(f32[2,12,32,128]{3,2,1,0:T(8,128)S(1)} %collective-permute-done.17.refs_0_), channel_id=1, source_target_pairs={{0,1},{1,0},{2,3},{3,2},{4,5},{5,4},{6,7},{7,6},{8,9},{9,8},{10,11... | collective-permute-start | bytes 1179656 | tf_op jit(solution)/shard_map/ppermute | solution.py:134
  133.3 13.7 %collective-permute-start.21 = (f32[12,32,128]{2,1,0:T(8,128)S(1)}, f32[12,32,128]{2,1,0:T(8,128)S(1)}, u32[]{:S(2)}, u32[]{:S(2)}) collective-permute-start(f32[12,32,128]{2,1,0:T(8,128)S(1)} %get-tuple-element.9), channel_id=1, source_target_pairs={{0,8},{1,9},{2,10},{3,11},{4,12},{5,13},{6,14},{7,15},{8,0},{9,1},... | collective-permute-start | bytes 589832 | tf_op jit(solution)/shard_map/ppermute | solution.py:134
  141.2 11.3 %collective-permute-start.23 = (f32[12,32,128]{2,1,0:T(8,128)S(1)}, f32[12,32,128]{2,1,0:T(8,128)S(1)}, u32[]{:S(2)}, u32[]{:S(2)}) collective-permute-start(f32[12,32,128]{2,1,0:T(8,128)S(1)} %get-tuple-element.10), channel_id=1, source_target_pairs={{0,24},{1,25},{2,26},{3,27},{4,28},{5,29},{6,30},{7,31},{8,16},{9,... | collective-permute-start | bytes 589832 | tf_op jit(solution)/shard_map/ppermute | solution.py:134
  143.3 10.6 %collective-permute-start.22 = (f32[12,32,128]{2,1,0:T(8,128)S(1)}, f32[12,32,128]{2,1,0:T(8,128)S(1)}, u32[]{:S(2)}, u32[]{:S(2)}) collective-permute-start(f32[12,32,128]{2,1,0:T(8,128)S(1)} %get-tuple-element.11), channel_id=1, source_target_pairs={{0,16},{1,17},{2,18},{3,19},{4,20},{5,21},{6,22},{7,23},{8,24},{9,... | collective-permute-start | bytes 589832 | tf_op jit(solution)/shard_map/ppermute | solution.py:134
